TPU v7x, 512 devices: a whole 4x8x8 slice. The times are simulated.
512 devices in a mesh: seq: 16 (over y_lo, z), clus: 32 (over x, y_hi, core).
Axes of the slice: x: 4, y: 8 (y_hi: 4, y_lo: 2; y = y_hi * 2 + y_lo), z: 8, core: 2. Of those that a mesh axis runs over, the one named last changes fastest.
Arguments:
- node_feats: bfloat16 [32, 2048, 1024], P('clus', 'seq'), may hold values from -24 to 24
- qkv_weight: bfloat16 [3072, 1024], P('seq'), may hold values from -1 to 1
- block_pairs: int32 [32, 128, 2], P('clus'), may hold values from 0 to 15, as said below
- grad_out: bfloat16 [32, 2048, 1024], P('clus', 'seq'), may hold values from -6 to 6
Outputs:
- attended: bfloat16 [32, 2048, 1024], P('clus', 'seq')
- node_grad: bfloat16 [32, 2048, 1024], P('clus', 'seq')
- weight_grad: float32 [3072, 1024], P('seq')
Inputs may be any that keep to these rules, and one draw needn't show every extreme that they name: `block_pairs`: each cluster's list holds 128 distinct pairs, among them (b, b) for every block b.
All inputs are finite; a program needn't handle non-finite values.
Results may differ from a plain program's by a relative error of at most 0.023.
Values may be sent and summed in bfloat16 or wider, within the bound.
A program may use at most 64 MiB of HBM per device.

v0:
```python
import math
import jax
import jax.numpy as jnp
from jax import lax
from jax.sharding import PartitionSpec as P

HD = 64
BLOCK = 128


def block_allowed(listed, blocks):
    block_ids = jnp.arange(blocks, dtype=jnp.int32)[None, :]
    row_hot = (listed[:, 0:1] == block_ids).astype(jnp.float32)
    col_hot = (listed[:, 1:2] == block_ids).astype(jnp.float32)
    counts = jnp.dot(row_hot.T, col_hot, precision=lax.Precision.HIGHEST)
    return counts > 0.5


def expand_rows(allowed_blocks, offset, row_span):
    picked = lax.dynamic_slice_in_dim(allowed_blocks, offset // BLOCK, row_span // BLOCK, 0)
    return jnp.repeat(jnp.repeat(picked, BLOCK, axis=0), BLOCK, axis=1)


def softmax_rows(query_rows, keys_all, allowed_rows):
    scores = jnp.einsum(
        "qhe,khe->hqk", query_rows, keys_all, preferred_element_type=jnp.float32
    ) * HD ** (-0.5)
    scores = jnp.where(allowed_rows[None], scores, -jnp.inf)
    row_max = jnp.max(scores, axis=-1, keepdims=True)
    unnorm = jnp.where(allowed_rows[None], jnp.exp(scores - row_max), 0.0)
    return unnorm / jnp.sum(unnorm, axis=-1, keepdims=True)


def local(node_feats, qkv_weight, block_pairs, grad_out):
    features = node_feats[0]
    rows_dev = features.shape[0]
    node_count = rows_dev * lax.axis_size("seq")
    columns = qkv_weight.shape[0]
    heads_dev = columns // (3 * HD)
    row_span = math.gcd(node_count, 512)
    offsets = jnp.arange(node_count // row_span, dtype=jnp.int32) * row_span
    projected = lax.dot_general(
        lax.all_gather(features, "seq", axis=0, tiled=True),
        qkv_weight,
        (((1,), (1,)), ((), ())),
        preferred_element_type=jnp.float32,
    ).astype(jnp.bfloat16)
    grouped = projected.reshape(node_count, heads_dev, 3, HD)
    queries = grouped[:, :, 0]
    keys_all = grouped[:, :, 1]
    values_all = grouped[:, :, 2]
    allowed_blocks = block_allowed(block_pairs[0], node_count // BLOCK)

    def forward_block(offset):
        query_rows = lax.dynamic_slice_in_dim(queries, offset, row_span, 0)
        weights = softmax_rows(query_rows, keys_all, expand_rows(allowed_blocks, offset, row_span))
        return jnp.einsum(
            "hqk,khe->qhe",
            weights.astype(jnp.bfloat16),
            values_all,
            preferred_element_type=jnp.float32,
        ).astype(jnp.bfloat16)

    head_out = lax.map(forward_block, offsets).reshape(node_count, heads_dev * HD)
    attended = lax.all_to_all(head_out, "seq", split_axis=0, concat_axis=1, tiled=True)
    upstream = lax.all_to_all(grad_out[0], "seq", split_axis=1, concat_axis=0, tiled=True).reshape(
        node_count, heads_dev, HD
    )

    def backward_block(state_pair, offset):
        grad_keys, grad_values = state_pair
        query_rows = lax.dynamic_slice_in_dim(queries, offset, row_span, 0)
        grad_rows = lax.dynamic_slice_in_dim(upstream, offset, row_span, 0)
        weights = softmax_rows(query_rows, keys_all, expand_rows(allowed_blocks, offset, row_span))
        weights_low = weights.astype(jnp.bfloat16)
        grad_weights = jnp.einsum(
            "qhe,khe->hqk", grad_rows, values_all, preferred_element_type=jnp.float32
        )
        row_delta = jnp.sum(weights * grad_weights, axis=-1, keepdims=True)
        grad_scores = (weights * (grad_weights - row_delta) * HD ** (-0.5)).astype(jnp.bfloat16)
        grad_query = jnp.einsum(
            "hqk,khe->qhe", grad_scores, keys_all, preferred_element_type=jnp.float32
        ).astype(jnp.bfloat16)
        grad_keys = grad_keys + jnp.einsum(
            "hqk,qhe->khe", grad_scores, query_rows, preferred_element_type=jnp.float32
        )
        grad_values = grad_values + jnp.einsum(
            "hqk,qhe->khe", weights_low, grad_rows, preferred_element_type=jnp.float32
        )
        return ((grad_keys, grad_values), grad_query)

    zeros_acc = jnp.zeros((node_count, heads_dev, HD), jnp.float32)
    sums_pair, grad_query = lax.scan(backward_block, (zeros_acc, zeros_acc), offsets)
    grad_query = grad_query.reshape(node_count, heads_dev, HD)
    grad_proj = jnp.stack(
        [grad_query, sums_pair[0].astype(jnp.bfloat16), sums_pair[1].astype(jnp.bfloat16)], axis=2
    ).reshape(node_count, columns)
    rows_part = grad_proj
    node_grad = lax.psum_scatter(
        jnp.dot(rows_part, qkv_weight, preferred_element_type=jnp.float32).astype(jnp.bfloat16),
        "seq",
        scatter_dimension=0,
        tiled=True,
    )
    rows_part = grad_proj
    local_sum = lax.dot_general(
        rows_part,
        lax.all_gather(features, "seq", axis=0, tiled=True),
        (((0,), (0,)), ((), ())),
        preferred_element_type=jnp.float32,
    )
    weight_grad = lax.psum(local_sum.astype(jnp.bfloat16), "clus").astype(
        jnp.float32
    ) / lax.axis_size("clus")
    return (attended[None], node_grad[None], weight_grad)


def solution(mesh):
    return jax.shard_map(
        local,
        mesh=mesh,
        in_specs=(
            P("clus", "seq", None),
            P("seq", None),
            P("clus", None, None),
            P("clus", "seq", None),
        ),
        out_specs=(P("clus", "seq", None), P("clus", "seq", None), P("seq", None)),
        check_vma=False,
    )
```

profile of v0, /device:TPU:6, one launch (start us, length us, event | category | flops | bytes accessed | tf_op | source)
XLA Modules:
  0.0 562.7 jit_solution(15509004296155294109)
XLA Ops:
  7.9 1.8 copy.19
  9.7 11.4 %all-to-all-start.1 = ((bf16[128,16,64]{0,2,1:T(8,128)(2,1)}), bf16[128,16,64]{0,2,1:T(8,128)(2,1)S(1)}, u32[]{:S(2)}, u32[]{:S(2)}) async-start(bf16[128,16,64]{0,2,1:T(8,128)(2,1)} %bitcast.19), calls=%async_computation.1 | async-start | bytes 524288 | tf_op jit(solution)/shard_map/all_to_all | solution.py:66
  22.2 9.6 %all-to-all-done.1 = bf16[128,16,64]{0,2,1:T(8,128)(2,1)S(1)} async-done(((bf16[128,16,64]{0,2,1:T(8,128)(2,1)}), bf16[128,16,64]{0,2,1:T(8,128)(2,1)S(1)}, u32[]{:S(2)}, u32[]{:S(2)}) %all-to-all-start.1) | async-done | bytes 262176 | tf_op jit(solution)/shard_map/all_to_all | solution.py:66
  32.8 61.0 %all-gather.3.cloned.1.call-done = bf16[1,2048,1024]{2,1,0:T(8,128)(2,1)} async-done(((bf16[1,128,1024]{2,1,0:T(8,128)(2,1)}), bf16[1,2048,1024]{2,1,0:T(8,128)(2,1)}) %all-gather.3.cloned.1.call-update) | async-done | bytes 4194320 | tf_op jit(solution)/shard_map/all_gather | solution.py:43
  93.8 3.7 fusion.44
  97.6 0.9 slice_bitcast_fusion
  99.2 88.3 %while.30 = (s32[]{:T(128)}, f32[2048,1,64]{0,2,1:T(8,128)S(1)}, f32[2048,1,64]{0,2,1:T(8,128)S(1)}, bf16[4,512,1,64]{1,3,2,0:T(8,128)(2,1)}, s32[4]{0:T(128)S(1...) while((s32[]{:T(128)}, f32[2048,1,64]{0,2,1:T(8,128)S(1)}, ...), condition=%wide.region_8.9_spmd.clone, body=%wide.region_4.8_spmd.clone.sunk | while | flops 692615680 | bytes 80837776 | solution.py:93
  102.1 3.5 broadcast_in_dim.122
  106.7 2.2 fusion.84
  108.8 1.4 fusion.85
  110.2 3.0 multiply_reduce_fusion.2
  113.3 2.0 copy-done.1
  115.8 1.6 fusion.86
  117.4 2.4 fusion.88
  119.8 1.5 fusion.87
  124.2 3.5 broadcast_in_dim.122
  128.8 2.2 fusion.84
  130.9 1.4 fusion.85
  132.3 3.0 multiply_reduce_fusion.2
  135.4 2.0 copy-done.1
  137.9 1.6 fusion.86
  139.5 2.4 fusion.88
  141.9 1.5 fusion.87
  146.3 3.5 broadcast_in_dim.122
  150.9 2.2 fusion.84
  153.0 1.4 fusion.85
  154.4 3.0 multiply_reduce_fusion.2
  157.5 2.0 copy-done.1
  160.0 1.6 fusion.86
  161.6 2.4 fusion.88
  164.0 1.5 fusion.87
  168.4 3.5 broadcast_in_dim.122
  173.0 2.2 fusion.84
  175.1 1.4 fusion.85
  176.5 3.0 multiply_reduce_fusion.2
  179.6 2.0 copy-done.1
  182.1 1.6 fusion.86
  183.7 2.4 fusion.88
  186.0 1.4 fusion.87
  187.5 1.2 copy.21
  189.0 3.9 fusion.47
  193.2 3.2 convolution_convert_fusion.1
  196.5 56.6 %while.29 = (s32[]{:T(128)}, bf16[4,512,1,64]{1,3,2,0:T(8,128)(2,1)S(1)}, s32[4]{0:T(128)S(1)}, pred[16,16]{1,0:T(8,128)(4,1)S(1)}, bf16[2048,1,64]{0,2,1:T(8,12...) while((s32[]{:T(128)}, ...), condition=%wide.region_3.4_spmd, body=%wide.region_0.3_spmd.sunk | while | flops 283147264 | bytes 17459756 | solution.py:64
  199.8 3.5 broadcast_in_dim.117
  204.5 2.2 fusion.75
  206.7 1.4 fusion.76
  208.1 2.6 fusion.77
  213.9 3.5 broadcast_in_dim.117
  218.7 2.2 fusion.75
  220.8 1.4 fusion.76
  222.2 2.6 fusion.77
  228.1 3.5 broadcast_in_dim.117
  232.8 2.2 fusion.75
  235.0 1.4 fusion.76
  236.4 2.6 fusion.77
  242.2 3.5 broadcast_in_dim.117
  247.0 2.2 fusion.75
  249.1 1.4 fusion.76
  250.5 2.6 fusion.77
  254.2 3.9 all-to-all-start
  258.1 203.0 %all-reduce.2.cloned.1.call-done = bf16[192,1024]{1,0:T(8,128)(2,1)} async-done(((bf16[192,1024]{1,0:T(8,128)(2,1)}), bf16[192,1024]{1,0:T(8,128)(2,1)}) %all-reduce.2.cloned.1.call-update) | async-done | bytes 393232 | tf_op jit(solution)/shard_map/psum | solution.py:112
  461.1 2.0 convert_multiply_fusion
  463.1 0.8 copy.22
  463.9 92.3 %reduce-scatter.2.cloned.1.call-done = bf16[128,1024]{1,0:T(8,128)(2,1)} async-done(((bf16[2048,1024]{1,0:T(8,128)(2,1)}), bf16[128,1024]{1,0:T(8,128)(2,1)}) %reduce-scatter.2.cloned.1.call-update) | async-done | bytes 262160 | tf_op jit(solution)/shard_map/reduce_scatter | solution.py:99
  (64 shorter events, 12.6 us)
Async XLA Ops:
  7.2 86.7 %copy-start = (bf16[192,1024]{1,0:T(8,128)(2,1)S(1)}, bf16[192,1024]{1,0:T(8,128)(2,1)}, u32[]{:S(2)}) copy-start(bf16[192,1024]{1,0:T(8,128)(2,1)} %param.9) | copy-start | bytes 1179652
  7.2 86.7 %all-gather.3.cloned.1.call-start = ((), (), s32[]{:S(2)}) async-start(), calls=%async_computation.5 | async-start | bytes 4456448 | tf_op jit(solution)/shard_map/all_gather | solution.py:43
  9.7 22.1 %all-to-all-start.1 = ((bf16[128,16,64]{0,2,1:T(8,128)(2,1)}), bf16[128,16,64]{0,2,1:T(8,128)(2,1)S(1)}, u32[]{:S(2)}, u32[]{:S(2)}) async-start(bf16[128,16,64]{0,2,1:T(8,128)(2,1)} %bitcast.19), calls=%async_computation.1 | async-start | bytes 524288 | tf_op jit(solution)/shard_map/all_to_all | solution.py:66
  21.1 439.9 %all-reduce.2.cloned.1.call-start = ((), (), s32[]{:S(2)}) async-start(), calls=%async_computation.4 | async-start | bytes 786432 | tf_op jit(solution)/shard_map/psum | solution.py:112
  113.3 2.0 copy-start.1
  115.8 4.0 copy-start.2
  135.4 2.0 copy-start.1
  137.9 4.0 copy-start.2
  157.5 2.0 copy-start.1
  160.0 4.0 copy-start.2
  179.6 2.0 copy-start.1
  182.1 4.0 copy-start.2
  192.9 363.3 %reduce-scatter.2.cloned.1.call-start = ((), (), s32[]{:S(2)}) async-start(), calls=%async_computation.3 | async-start | bytes 4456448 | tf_op jit(solution)/shard_map/reduce_scatter | solution.py:99
  254.2 208.8 %all-to-all-start = ((bf16[16,128,64]{1,2,0:T(8,128)(2,1)}), bf16[16,128,64]{1,2,0:T(8,128)(2,1)S(1)}, u32[]{:S(2)}, u32[]{:S(2)}) async-start(bf16[16,128,64]{1,2,0:T(8,128)(2,1)} %copy.18), calls=%async_computation | async-start | bytes 524288 | tf_op jit(solution)/shard_map/all_to_all | solution.py:65
Sparse Core Ops, SparseCore 0:
  10.1 83.7 all-gather.2
  193.1 267.9 all-reduce.1
  464.5 91.6 reduce-scatter.1
where the time goes:
time: 564 us; the launch traced here: 563 us
  waiting for transfers between devices  367 us (65%)
  matrix products  72.6 us (13%)
  local copies, waits for them, and re-layouts  49.3 us (9%)
  loops' own time  29.3 us (5%)
  starting transfers between devices  15.6 us (3%)
  other arithmetic  15.5 us (3%)
  between operations  13.9 us (2%)
    psum x1, waiting for transfers between devices, local(): lax.psum(local_sum.astype(jnp.bfloat16), 'clus').astype(jnp.float32)  203 us
    reduce_scatter x1, waiting for transfers between devices, local(): lax.psum_scatter(jnp.dot(rows_part, qkv_weight, preferred_element_type=jn...  92.3 us
    all_gather x1, waiting for transfers between devices, local(): lax.all_gather(features, 'seq', axis=0, tiled=True)  61 us
    broadcast_in_dim x16, local copies, waits for them, and re-layouts, expand_rows(): return jnp.repeat(jnp.repeat(picked, BLOCK, axis=0), BLOCK, axis=1)  27.9 us
    dot_general x8, matrix products, softmax_rows(): jnp.einsum('qhe,khe->hqk', query_rows, keys_all, preferred_element_type=j...  17.3 us
    another operation x1, loops' own time, local(): lax.map(forward_block, offsets).reshape(node_count, heads_dev * HD)  15.5 us
    another operation x1, loops' own time, local(): lax.scan(backward_block, (zeros_acc, zeros_acc), offsets)  13.8 us
    dot_general x4, matrix products, backward_block(): jnp.einsum('qhe,khe->hqk', grad_rows, values_all, preferred_element_type=...  12.1 us
  transfers between devices with their start and end apart: 5, of which 4 were waited for; matrix products, arithmetic and copies ran while one was open for 9% of the time, Pallas kernels for 0%

commit v1 on v0

--- a/solution.py
+++ b/solution.py
@@ -109,7 +109,7 @@
         (((0,), (0,)), ((), ())),
         preferred_element_type=jnp.float32,
     )
-    weight_grad = lax.psum(local_sum.astype(jnp.bfloat16), "clus").astype(
+    weight_grad = jnp.sum(lax.all_gather(local_sum.astype(jnp.bfloat16), "clus"), axis=0).astype(
         jnp.float32
     ) / lax.axis_size("clus")
     return (attended[None], node_grad[None], weight_grad)

time: 564 us -> 396 us (0.70)
  waiting for transfers between devices: 367 us -> 171 us
  blocking collectives: 0 us -> 19.7 us
  other arithmetic: 15.5 us -> 22.3 us
    psum x1 -> x0, waiting for transfers between devices: 203 us -> none  [local(): lax.psum(local_sum.astype(jnp.bfloat16), 'clus').astype(jnp.float32)]
    all_gather x0 -> x1, waiting for transfers between devices: none -> 21.1 us  [local(): lax.all_gather(local_sum.astype(jnp.bfloat16), 'clus')]
    all_to_all x0 -> x1, blocking collectives: none -> 19.7 us  [local(): lax.all_to_all(head_out, 'seq', split_axis=0, concat_axis=1, tiled=True)]
    reduce_scatter x1, waiting for transfers between devices: 92.3 us -> 78.9 us  [local(): lax.psum_scatter(jnp.dot(rows_part, qkv_weight, preferred_element_type=jn...]
    reduce_sum x0 -> x1, other arithmetic: none -> 7.87 us  [local(): jnp.sum(lax.all_gather(local_sum.astype(jnp.bfloat16), 'clus'), axis=0)]
  transfers between devices with their start and end apart: 5 -> 4, of which waited for: 4 -> 4; matrix products, arithmetic and copies ran while one was open for 9% -> 15% of each run, Pallas kernels for 0% -> 0%
where the time goes in v1:
time: 396 us; the launch traced here: 394 us
  waiting for transfers between devices  171 us (43%)
  matrix products  72.7 us (18%)
  local copies, waits for them, and re-layouts  49 us (12%)
  loops' own time  33.8 us (9%)
  other arithmetic  22.3 us (6%)
  blocking collectives  19.7 us (5%)
  between operations  13.9 us (4%)
  starting transfers between devices  11.7 us (3%)
    reduce_scatter x1, waiting for transfers between devices, local(): lax.psum_scatter(jnp.dot(rows_part, qkv_weight, preferred_element_type=jn...  78.9 us
    all_gather x1, waiting for transfers between devices, local(): lax.all_gather(features, 'seq', axis=0, tiled=True)  61 us
    broadcast_in_dim x16, local copies, waits for them, and re-layouts, expand_rows(): return jnp.repeat(jnp.repeat(picked, BLOCK, axis=0), BLOCK, axis=1)  27.9 us
    all_gather x1, waiting for transfers between devices, local(): lax.all_gather(local_sum.astype(jnp.bfloat16), 'clus')  21.1 us
    all_to_all x1, blocking collectives, local(): lax.all_to_all(head_out, 'seq', split_axis=0, concat_axis=1, tiled=True)  19.7 us
    dot_general x8, matrix products, softmax_rows(): jnp.einsum('qhe,khe->hqk', query_rows, keys_all, preferred_element_type=j...  17.3 us
    another operation x1, loops' own time, local(): lax.scan(backward_block, (zeros_acc, zeros_acc), offsets)  17 us
    another operation x1, loops' own time, local(): lax.map(forward_block, offsets).reshape(node_count, heads_dev * HD)  16.8 us
  transfers between devices with their start and end apart: 4, of which 4 were waited for; matrix products, arithmetic and copies ran while one was open for 15% of the time, Pallas kernels for 0%

profile of v1, /device:TPU:6, one launch (start us, length us, event | category | flops | bytes accessed | tf_op | source)
XLA Modules:
  0.0 394.4 jit_solution(14721656960751760977)
XLA Ops:
  7.9 1.8 copy.19
  9.7 11.4 %all-to-all-start.1 = ((bf16[128,16,64]{0,2,1:T(8,128)(2,1)}), bf16[128,16,64]{0,2,1:T(8,128)(2,1)S(1)}, u32[]{:S(2)}, u32[]{:S(2)}) async-start(bf16[128,16,64]{0,2,1:T(8,128)(2,1)} %bitcast.19), calls=%async_computation.1 | async-start | bytes 524288 | tf_op jit(solution)/shard_map/all_to_all | solution.py:66
  22.2 9.6 %all-to-all-done.1 = bf16[128,16,64]{0,2,1:T(8,128)(2,1)S(1)} async-done(((bf16[128,16,64]{0,2,1:T(8,128)(2,1)}), bf16[128,16,64]{0,2,1:T(8,128)(2,1)S(1)}, u32[]{:S(2)}, u32[]{:S(2)}) %all-to-all-start.1) | async-done | bytes 262176 | tf_op jit(solution)/shard_map/all_to_all | solution.py:66
  32.8 61.0 %all-gather.5.cloned.1.call-done = bf16[1,2048,1024]{2,1,0:T(8,128)(2,1)} async-done(((bf16[1,128,1024]{2,1,0:T(8,128)(2,1)}), bf16[1,2048,1024]{2,1,0:T(8,128)(2,1)}) %all-gather.5.cloned.1.call-update) | async-done | bytes 4194320 | tf_op jit(solution)/shard_map/all_gather | solution.py:43
  93.8 3.7 fusion.44
  97.6 0.9 slice_bitcast_fusion
  99.2 91.8 %while.30 = (s32[]{:T(128)}, f32[2048,1,64]{0,2,1:T(8,128)S(1)}, f32[2048,1,64]{0,2,1:T(8,128)S(1)}, bf16[4,512,1,64]{1,3,2,0:T(8,128)(2,1)}, s32[4]{0:T(128)S(1...) while((s32[]{:T(128)}, f32[2048,1,64]{0,2,1:T(8,128)S(1)}, ...), condition=%wide.region_8.9_spmd.clone, body=%wide.region_4.8_spmd.clone.sunk | while | flops 692615680 | bytes 80837776 | solution.py:93
  102.7 3.5 broadcast_in_dim.122
  107.5 2.2 fusion.84
  109.7 1.4 fusion.85
  111.1 3.0 multiply_reduce_fusion.2
  114.1 2.0 copy-done.1
  116.6 1.6 fusion.86
  118.3 2.4 fusion.88
  120.6 1.5 fusion.87
  125.6 3.5 broadcast_in_dim.122
  130.5 2.2 fusion.84
  132.6 1.4 fusion.85
  134.0 3.0 multiply_reduce_fusion.2
  137.1 2.0 copy-done.1
  139.6 1.6 fusion.86
  141.3 2.4 fusion.88
  143.6 1.5 fusion.87
  148.6 3.5 broadcast_in_dim.122
  153.5 2.2 fusion.84
  155.6 1.4 fusion.85
  157.0 3.0 multiply_reduce_fusion.2
  160.1 2.0 copy-done.1
  162.6 1.6 fusion.86
  164.2 2.4 fusion.88
  166.6 1.5 fusion.87
  171.6 3.5 broadcast_in_dim.122
  176.4 2.2 fusion.84
  178.6 1.4 fusion.85
  180.0 3.0 multiply_reduce_fusion.2
  183.0 2.0 copy-done.1
  185.5 1.6 fusion.86
  187.1 2.4 fusion.88
  189.5 1.4 fusion.87
  190.9 1.2 copy.21
  192.4 3.9 fusion.47
  196.6 3.3 convolution_convert_fusion.1
  199.9 58.1 %while.29 = (s32[]{:T(128)}, bf16[4,512,1,64]{1,3,2,0:T(8,128)(2,1)S(1)}, s32[4]{0:T(128)S(1)}, pred[16,16]{1,0:T(8,128)(4,1)S(1)}, bf16[2048,1,64]{0,2,1:T(8,12...) while((s32[]{:T(128)}, ...), condition=%wide.region_3.4_spmd, body=%wide.region_0.3_spmd.sunk | while | flops 283147264 | bytes 17459756 | solution.py:64
  203.4 3.5 broadcast_in_dim.117
  208.3 2.2 fusion.75
  210.5 1.4 fusion.76
  211.9 2.6 fusion.77
  218.0 3.5 broadcast_in_dim.117
  222.8 2.2 fusion.75
  225.0 1.4 fusion.76
  226.4 2.6 fusion.77
  232.5 3.5 broadcast_in_dim.117
  237.3 2.2 fusion.75
  239.5 1.4 fusion.76
  240.9 2.6 fusion.77
  247.1 3.5 broadcast_in_dim.117
  251.9 2.2 fusion.75
  254.1 1.4 fusion.76
  255.5 2.6 fusion.77
  258.5 19.7 %all_to_all.32 = bf16[16,128,64]{1,2,0:T(8,128)(2,1)S(1)} all-to-all(bf16[16,128,64]{1,2,0:T(8,128)(2,1)S(1)} %copy.18), channel_id=1, replica_groups=mesh['seq'=16,'clus'=32] {'seq'}, dimensions={0} | all-to-all | bytes 524288 | tf_op jit(solution)/shard_map/all_to_all | solution.py:65
  279.0 21.1 %all-gather.7.cloned.1.call-done = bf16[6144,1024]{1,0:T(8,128)(2,1)} async-done(((bf16[192,1024]{1,0:T(8,128)(2,1)}), bf16[6144,1024]{1,0:T(8,128)(2,1)}) %all-gather.7.cloned.1.call-update) | async-done | bytes 12582928 | tf_op jit(solution)/shard_map/all_gather | solution.py:112
  300.1 7.9 %reduce_sum.39 = bf16[192,1024]{1,0:T(8,128)(2,1)S(1)} reduce(bf16[32,192,1024]{2,1,0:T(8,128)(2,1)} %bitcast.212, bf16[]{:T(256)} %constant.141.clone.1), dimensions={0}, to_apply=%region_10.11 | reduce | flops 6094848 | bytes 12976130 | tf_op jit(solution)/shard_map/reduce_sum | solution.py:112
  308.0 1.0 convert_multiply_fusion
  308.9 78.9 %reduce-scatter.2.cloned.1.call-done = bf16[128,1024]{1,0:T(8,128)(2,1)} async-done(((bf16[2048,1024]{1,0:T(8,128)(2,1)}), bf16[128,1024]{1,0:T(8,128)(2,1)}) %reduce-scatter.2.cloned.1.call-update) | async-done | bytes 262160 | tf_op jit(solution)/shard_map/reduce_scatter | solution.py:99
  (64 shorter events, 13.2 us)
Async XLA Ops:
  7.2 86.7 %copy-start = (bf16[192,1024]{1,0:T(8,128)(2,1)S(1)}, bf16[192,1024]{1,0:T(8,128)(2,1)}, u32[]{:S(2)}) copy-start(bf16[192,1024]{1,0:T(8,128)(2,1)} %param.9) | copy-start | bytes 1179652
  7.2 86.7 %all-gather.5.cloned.1.call-start = ((), (), s32[]{:S(2)}) async-start(), calls=%async_computation.4 | async-start | bytes 4456448 | tf_op jit(solution)/shard_map/all_gather | solution.py:43
  9.7 22.1 %all-to-all-start.1 = ((bf16[128,16,64]{0,2,1:T(8,128)(2,1)}), bf16[128,16,64]{0,2,1:T(8,128)(2,1)S(1)}, u32[]{:S(2)}, u32[]{:S(2)}) async-start(bf16[128,16,64]{0,2,1:T(8,128)(2,1)} %bitcast.19), calls=%async_computation.1 | async-start | bytes 524288 | tf_op jit(solution)/shard_map/all_to_all | solution.py:66
  21.1 278.9 %all-gather.7.cloned.1.call-start = ((), (), s32[]{:S(2)}) async-start(), calls=%async_computation.5 | async-start | bytes 12976128 | tf_op jit(solution)/shard_map/all_gather | solution.py:112
  114.1 2.0 copy-start.1
  116.6 4.0 %copy-start.2 = (f32[512,2048]{1,0:T(8,128)S(1)}, f32[512,2048]{1,0:T(8,128)}, u32[]{:S(2)}) copy-start(f32[512,2048]{1,0:T(8,128)} %copy-done.1) | copy-start | bytes 12582916 | tf_op jit(solution)/shard_map/while
  137.1 2.0 copy-start.1
  139.6 4.0 %copy-start.2 = (f32[512,2048]{1,0:T(8,128)S(1)}, f32[512,2048]{1,0:T(8,128)}, u32[]{:S(2)}) copy-start(f32[512,2048]{1,0:T(8,128)} %copy-done.1) | copy-start | bytes 12582916 | tf_op jit(solution)/shard_map/while
  160.1 2.0 copy-start.1
  162.6 4.0 %copy-start.2 = (f32[512,2048]{1,0:T(8,128)S(1)}, f32[512,2048]{1,0:T(8,128)}, u32[]{:S(2)}) copy-start(f32[512,2048]{1,0:T(8,128)} %copy-done.1) | copy-start | bytes 12582916 | tf_op jit(solution)/shard_map/while
  183.0 2.0 copy-start.1
  185.5 4.0 %copy-start.2 = (f32[512,2048]{1,0:T(8,128)S(1)}, f32[512,2048]{1,0:T(8,128)}, u32[]{:S(2)}) copy-start(f32[512,2048]{1,0:T(8,128)} %copy-done.1) | copy-start | bytes 12582916 | tf_op jit(solution)/shard_map/while
  196.4 191.5 %reduce-scatter.2.cloned.1.call-start = ((), (), s32[]{:S(2)}) async-start(), calls=%async_computation.3 | async-start | bytes 4456448 | tf_op jit(solution)/shard_map/reduce_scatter | solution.py:99
Sparse Core Ops, SparseCore 0:
  10.1 83.7 all-gather.4
  196.5 103.5 all-gather.6
  303.5 84.3 reduce-scatter.1
